TPU v7x, 256 devices: a whole 4x4x8 slice. The times are simulated.
256 devices in a mesh: view: 16 (over z, x_hi), row: 4 (over x_lo, core), col: 4 (over y).
Axes of the slice: x: 4 (x_hi: 2, x_lo: 2; x = x_hi * 2 + x_lo), y: 4, z: 8, core: 2. Of those that a mesh axis runs over, the one named last changes fastest.
Arguments:
- residual: bfloat16 [16, 32, 128, 1024], P('view', 'row', 'col'), may hold values from -6 to 6
- window_query: bfloat16 [16, 32, 128, 1024], P('view', 'row', 'col'), may hold values from -56 to 56
- window_pairs: bfloat16 [2, 16, 32, 128, 1024], P(None, 'view', 'row', 'col'), may hold values from -4 to 4
- near_output: bfloat16 [1024, 1024], P('view'), may hold values from -0.1875 to 0.1875
- norm_gain: float32 [1024], replicated, may hold values from 0.1 to 1.9
- cross_input: bfloat16 [1024, 3072], P('view'), may hold values from -0.125 to 0.125
- head_gain: float32 [2, 64], replicated, may hold values from 0.7 to 6
- cross_output: bfloat16 [1024, 1024], P('view'), may hold values from -0.1875 to 0.1875
Outputs:
- block_out: bfloat16 [16, 32, 128, 1024], P('view', 'row', 'col')
All inputs are finite; a program needn't handle non-finite values.
Results may differ from a plain program's by a relative error of at most 0.018.
Values may be sent and summed in bfloat16 or wider, within the bound.
A program may use at most 128 MiB of HBM per device.

v0:
```python
import jax
import jax.numpy as jnp
from jax import lax
from jax.sharding import PartitionSpec as P

HEAD_DIM = 64
WINDOW = 13
RADIUS = 6


def padded(block, sides, width):
    for axis, dim in sides:
        count = lax.axis_size(axis)
        forward = [(i, i + 1) for i in range(count - 1)]
        backward = [(target, source) for source, target in forward]
        low = lax.ppermute(
            lax.slice_in_dim(block, block.shape[dim] - width, None, axis=dim), axis, forward
        )
        high = lax.ppermute(lax.slice_in_dim(block, 0, width, axis=dim), axis, backward)
        block = jnp.concatenate([low, block, high], axis=dim)
    return block


def window_mask(span_count, offset, total):
    queried = offset + jnp.arange(span_count, dtype=jnp.int32)
    keyed = offset - RADIUS + jnp.arange(span_count + 2 * RADIUS, dtype=jnp.int32)
    first_at = jnp.clip(queried - RADIUS, 0, total - WINDOW)
    return (keyed[None, :] >= first_at[:, None]) & (
        keyed[None, :] <= first_at[:, None] + WINDOW - 1
    )


def both_masks(tile_rows, tile_cols, row_start, col_start, row_count, col_count):
    by_row = window_mask(tile_rows, row_start, row_count)
    by_col = window_mask(tile_cols, col_start, col_count)
    joined = by_row[:, None, :, None] & by_col[None, :, None, :]
    return joined.reshape(
        tile_rows * tile_cols, (tile_rows + 2 * RADIUS) * (tile_cols + 2 * RADIUS)
    )


def neighborhood(queries, key_tile, value_tile, allowed):
    token_count = queries.shape[0] * queries.shape[1]
    span_total = key_tile.shape[0] * key_tile.shape[1]
    features = queries.shape[2]
    head_count = features // HEAD_DIM
    query_heads = queries.reshape(token_count, head_count, HEAD_DIM).transpose(1, 0, 2)
    key_heads = key_tile.reshape(span_total, head_count, HEAD_DIM).transpose(1, 0, 2)
    value_heads = value_tile.reshape(span_total, head_count, HEAD_DIM).transpose(1, 0, 2)

    def one_head(pieces):
        query_h, key_h, value_h = pieces
        scores = jnp.dot(query_h, key_h.T, preferred_element_type=jnp.float32) * HEAD_DIM ** (-0.5)
        scores = jnp.where(allowed, scores, -jnp.inf)
        highest = jnp.max(scores, axis=1, keepdims=True)
        exponent = jnp.exp(scores - highest)
        summed = jnp.sum(exponent, axis=1, keepdims=True)
        mixture = jnp.dot(
            exponent.astype(jnp.bfloat16), value_h, preferred_element_type=jnp.float32
        )
        return (mixture / summed).astype(jnp.bfloat16)

    result = lax.map(one_head, (query_heads, key_heads, value_heads))
    return result.transpose(1, 0, 2).reshape(token_count, features)


def rms_scale(values, gain_vec, epsilon):
    meansq = jnp.mean(values * values, axis=-1, keepdims=True)
    return values * lax.rsqrt(meansq + epsilon) * gain_vec


def split_projected(projected, head_gain, features):
    token_count = projected.shape[0]
    head_count = features // HEAD_DIM
    queried = rms_scale(
        projected[:, :features].reshape(token_count, head_count, HEAD_DIM), head_gain[0], 1e-06
    )
    keyed = rms_scale(
        projected[:, features : 2 * features].reshape(token_count, head_count, HEAD_DIM),
        head_gain[1],
        1e-06,
    )
    return (
        queried.astype(jnp.bfloat16).reshape(token_count, features),
        keyed.astype(jnp.bfloat16).reshape(token_count, features),
        projected[:, 2 * features :].astype(jnp.bfloat16),
    )


def across(queries, key_views, value_views):
    view_count, token_count, features = queries.shape
    other_count = key_views.shape[0]
    head_count = features // HEAD_DIM
    queried = queries.reshape(view_count, token_count, head_count, HEAD_DIM)
    keyed = key_views.reshape(other_count, token_count, head_count, HEAD_DIM)
    valued = value_views.reshape(other_count, token_count, head_count, HEAD_DIM)
    scores = jnp.einsum(
        "vnhd,wnhd->nhvw", queried, keyed, preferred_element_type=jnp.float32
    ) * HEAD_DIM ** (-0.5)
    highest = jnp.max(scores, axis=3, keepdims=True)
    exponent = jnp.exp(scores - highest)
    summed = jnp.sum(exponent, axis=3)
    mixture = jnp.einsum(
        "nhvw,wnhd->vnhd", exponent.astype(jnp.bfloat16), valued, preferred_element_type=jnp.float32
    )
    mixture = mixture / jnp.transpose(summed, (2, 0, 1))[..., None]
    return mixture.astype(jnp.bfloat16).reshape(view_count, token_count, features)


def row_folder(left_rows, piece):
    return jnp.dot(left_rows, piece, preferred_element_type=jnp.float32)


def attend_pixels(pieces):
    query_part, pair_part = pieces
    return across(query_part[0, :, 0], pair_part[0, :, 0], pair_part[1, :, 0])


def local(
    residual,
    window_query,
    window_pairs,
    near_output,
    norm_gain,
    cross_input,
    head_gain,
    cross_output,
):
    tile_rows = residual.shape[1]
    tile_cols = residual.shape[2]
    features = residual.shape[3]
    token_count = tile_rows * tile_cols
    groups = lax.axis_size("view")
    group_len = token_count // groups
    nearby = padded(window_pairs, (("row", 2), ("col", 3)), RADIUS)
    row_start = lax.axis_index("row") * tile_rows
    col_start = lax.axis_index("col") * tile_cols
    allowed = both_masks(
        tile_rows,
        tile_cols,
        row_start,
        col_start,
        tile_rows * lax.axis_size("row"),
        tile_cols * lax.axis_size("col"),
    )
    attended = neighborhood(window_query[0], nearby[0, 0], nearby[1, 0], allowed)
    near_term = row_folder(attended, lax.all_gather(near_output, "view", axis=0, tiled=True))
    residue = residual[0].reshape(token_count, features)
    hidden = (residue.astype(jnp.float32) + near_term).astype(jnp.bfloat16)
    normed = rms_scale(hidden.astype(jnp.float32), norm_gain, 1e-05).astype(jnp.bfloat16)
    projected = row_folder(normed, lax.all_gather(cross_input, "view", axis=0, tiled=True))
    queried, keyed, valued = split_projected(projected, head_gain, features)
    query_block = queried.reshape(1, 1, groups, group_len, features)
    pair_block = jnp.stack([keyed, valued]).reshape(2, 1, groups, group_len, features)
    mixture = attend_pixels(
        (
            lax.all_to_all(query_block, "view", split_axis=2, concat_axis=1, tiled=True),
            lax.all_to_all(pair_block, "view", split_axis=2, concat_axis=1, tiled=True),
        )
    )
    returned = lax.all_to_all(mixture, "view", split_axis=0, concat_axis=1, tiled=True)
    crossed = returned[0]
    cross_term = row_folder(crossed, lax.all_gather(cross_output, "view", axis=0, tiled=True))
    block_out = (hidden.astype(jnp.float32) + cross_term).astype(jnp.bfloat16)
    return block_out.reshape(1, tile_rows, tile_cols, features)


def solution(mesh):
    in_specs = (
        P("view", "row", "col", None),
        P("view", "row", "col", None),
        P(None, "view", "row", "col", None),
        P("view", None),
        P(),
        P("view", None),
        P(),
        P("view", None),
    )
    out_specs = P("view", "row", "col", None)
    return jax.shard_map(local, mesh=mesh, in_specs=in_specs, out_specs=out_specs, check_vma=False)
```

profile of v0, /device:TPU:1, one launch (start us, length us, event | category | flops | bytes accessed | tf_op | source)
XLA Modules:
  0.0 352.9 jit_solution(18072664135709869636)
XLA Ops:
  7.3 2.7 fusion.42
  10.0 4.5 %collective-permute-start = (bf16[2,1,6,32,1024]{4,3,2,1,0:T(8,128)(2,1)}, bf16[2,1,6,32,1024]{4,3,2,1,0:T(8,128)(2,1)S(1)}, u32[]{:S(2)}, u32[]{:S(2)}) collective-permute-start(bf16[2,1,6,32,1024]{4,3,2,1,0:T(8,128)(2,1)} %get-tuple-element.103), channel_id=1, source_target_pairs={{0,4},{4,8},{8,12},{1,5},{5,9},{9,13},{2,6},{6,10},{10,14},{3,7},{... | collective-permute-start | bytes 2359304 | tf_op jit(solution)/shard_map/ppermute | solution.py:16
  14.5 2.0 collective-permute-start.1
  17.2 6.5 %collective-permute-done = bf16[2,1,6,32,1024]{4,3,2,1,0:T(8,128)(2,1)S(1)} collective-permute-done((bf16[2,1,6,32,1024]{4,3,2,1,0:T(8,128)(2,1)}, bf16[2,1,6,32,1024]{4,3,2,1,0:T(8,128)(2,1)S(1)}, u32[]{:S(2)}, u32[]{:S(2)}) %collective-permute-start) | collective-permute-done | bytes 786464 | tf_op jit(solution)/shard_map/ppermute | solution.py:16
  24.2 4.0 %collective-permute-done.1 = bf16[2,1,6,32,1024]{4,3,2,1,0:T(8,128)(2,1)} collective-permute-done((bf16[2,1,6,32,1024]{4,3,2,1,0:T(8,128)(2,1)}, bf16[2,1,6,32,1024]{4,3,2,1,0:T(8,128)(2,1)}, u32[]{:S(2)}, u32[]{:S(2)}) %collective-permute-start.1) | collective-permute-done | bytes 786464 | tf_op jit(solution)/shard_map/ppermute | solution.py:19
  29.7 1.7 pad_maximum_fusion.4
  31.4 4.3 %collective-permute-start.2 = (bf16[2,1,20,6,1024]{4,2,3,1,0:T(8,128)(2,1)}, bf16[2,1,20,6,1024]{4,2,3,1,0:T(8,128)(2,1)}, u32[]{:S(2)}, u32[]{:S(2)}) collective-permute-start(bf16[2,1,20,6,1024]{4,2,3,1,0:T(8,128)(2,1)} %get-tuple-element.99), channel_id=1, source_target_pairs={{0,1},{1,2},{2,3},{4,5},{5,6},{6,7},{8,9},{9,10},{10,11},{12,13},{... | collective-permute-start | bytes 1474568 | tf_op jit(solution)/shard_map/ppermute | solution.py:16
  37.2 2.5 reshape_squeeze.19
  39.7 2.5 copy.47
  42.4 4.5 %collective-permute-done.3 = bf16[2,1,20,6,1024]{4,2,3,1,0:T(8,128)(2,1)} collective-permute-done((bf16[2,1,20,6,1024]{4,2,3,1,0:T(8,128)(2,1)}, bf16[2,1,20,6,1024]{4,2,3,1,0:T(8,128)(2,1)}, u32[]{:S(2)}, u32[]{:S(2)}) %collective-permute-start.3) | collective-permute-done | bytes 491552 | tf_op jit(solution)/shard_map/ppermute | solution.py:19
  46.9 2.9 pad_maximum_fusion
  50.3 2.3 copy.45
  52.5 6.0 %reshape_squeeze.20 = bf16[880,16,64]{2,1,0:T(8,128)(2,1)} reshape(bf16[1,1,20,44,1024]{4,3,2,1,0:T(8,128)(2,1)} %copy.45) | data formatting | bytes 3604480 | tf_op jit(solution)/shard_map/reshape;squeeze | solution.py:48
  58.5 4.8 %copy.48 = bf16[16,880,64]{2,1,0:T(8,128)(2,1)} copy(bf16[16,880,64]{2,0,1:T(8,128)(2,1)} %bitcast.74) | data formatting | bytes 3604480
  63.3 2.3 copy.46
  65.6 5.9 %reshape_squeeze.21 = bf16[880,16,64]{2,1,0:T(8,128)(2,1)} reshape(bf16[1,1,20,44,1024]{4,3,2,1,0:T(8,128)(2,1)} %copy.46) | data formatting | bytes 3604480 | tf_op jit(solution)/shard_map/reshape;squeeze | solution.py:49
  71.5 4.9 %copy.49 = bf16[16,880,64]{2,1,0:T(8,128)(2,1)} copy(bf16[16,880,64]{2,0,1:T(8,128)(2,1)} %bitcast.75) | data formatting | bytes 3604480
  76.5 73.5 %while.11 = (s32[]{:T(128)}, bf16[16,256,64]{1,2,0:T(8,128)(2,1)S(1)}, bf16[16,256,64]{2,1,0:T(8,128)(2,1)}, bf16[16,880,64]{2,1,0:T(8,128)(2,1)}, bf16[16,880,6...) while((s32[]{:T(128)}, ...), condition=%wide.region_3.4_spmd.clone, body=%wide.region_0.3_spmd.clone.sunk | while | flops 59506176 | bytes 4612725 | solution.py:63
  150.0 2.5 fusion.23
  152.6 61.3 %all-gather.6.cloned.1.call-done = bf16[1024,3072]{1,0:T(8,128)(2,1)} async-done(((bf16[64,3072]{1,0:T(8,128)(2,1)}), bf16[1024,3072]{1,0:T(8,128)(2,1)}) %all-gather.6.cloned.1.call-update) | async-done | bytes 6291472 | tf_op jit(solution)/shard_map/all_gather | solution.py:151
  213.8 4.7 %fusion.34 = f32[256,3072]{1,0:T(8,128)S(1)} fusion(bf16[1024,3072]{1,0:T(8,128)(2,1)} %all-gather.6.cloned.1.call-done, bf16[256,1024]{1,0:T(8,128)(2,1)S(1)} %get-tuple-element.108, f32[1024]{0:T(1024)S(1)} %copy-done.10, f32[256]{0:T(256)S(1)} %add_rsqrt_fusion.2), kind=kOutput, calls=%fused_computation.52 | convolution fusion | flops 1611661312 | bytes 9966592 | tf_op jit(solution)/shard_map/dot_general | solution.py:111
  218.5 2.1 slice_multiply_fusion
  222.8 2.3 fusion.33
  225.1 4.4 %all-to-all-start.1 = ((bf16[1,1,16,16,1024]{4,3,1,0,2:T(8,128)(2,1)}), bf16[1,1,16,16,1024]{4,3,1,0,2:T(8,128)(2,1)}, u32[]{:S(2)}, u32[]{:S(2)}) async-start(bf16[1,1,16,16,1024]{4,3,1,0,2:T(8,128)(2,1)} %fusion.33), calls=%async_computation.1 | async-start | bytes 1048576 | tf_op jit(solution)/shard_map/all_to_all | solution.py:157
  229.6 2.1 slice.68
  236.1 9.9 %all-to-all-done.1 = bf16[1,1,16,16,1024]{4,3,1,0,2:T(8,128)(2,1)} async-done(((bf16[1,1,16,16,1024]{4,3,1,0,2:T(8,128)(2,1)}), bf16[1,1,16,16,1024]{4,3,1,0,2:T(8,128)(2,1)}, u32[]{:S(2)}, u32[]{:S(2)}) %all-to-all-start.1) | async-done | bytes 524320 | tf_op jit(solution)/shard_map/all_to_all | solution.py:157
  246.0 4.3 %all-to-all-start = ((bf16[2,1,16,16,1024]{4,3,1,0,2:T(8,128)(2,1)}), bf16[2,1,16,16,1024]{4,3,1,0,2:T(8,128)(2,1)S(1)}, u32[]{:S(2)}, u32[]{:S(2)}) async-start(bf16[2,1,16,16,1024]{4,3,1,0,2:T(8,128)(2,1)} %copy.52), calls=%async_computation | async-start | bytes 2097152 | tf_op jit(solution)/shard_map/all_to_all | solution.py:158
  251.1 2.0 reshape_squeeze.23
  253.1 23.4 %all-to-all-done = bf16[2,1,16,16,1024]{4,3,1,0,2:T(8,128)(2,1)S(1)} async-done(((bf16[2,1,16,16,1024]{4,3,1,0,2:T(8,128)(2,1)}), bf16[2,1,16,16,1024]{4,3,1,0,2:T(8,128)(2,1)S(1)}, u32[]{:S(2)}, u32[]{:S(2)}) %all-to-all-start) | async-done | bytes 1048608 | tf_op jit(solution)/shard_map/all_to_all | solution.py:158
  284.9 6.7 %all-to-all-start.2 = ((bf16[16,16,1024]{2,1,0:T(8,128)(2,1)}), bf16[16,16,1024]{2,1,0:T(8,128)(2,1)S(1)}, u32[]{:S(2)}, u32[]{:S(2)}) async-start(bf16[16,16,1024]{2,1,0:T(8,128)(2,1)} %reshape.267), calls=%async_computation.2 | async-start | bytes 1048576 | tf_op jit(solution)/shard_map/all_to_all | solution.py:161
  291.6 51.6 %all-gather.8.cloned.1.call-done = bf16[1024,1024]{1,0:T(8,128)(2,1)} async-done(((bf16[64,1024]{1,0:T(8,128)(2,1)}), bf16[1024,1024]{1,0:T(8,128)(2,1)}) %all-gather.8.cloned.1.call-update) | async-done | bytes 2097168 | tf_op jit(solution)/shard_map/all_gather | solution.py:163
  343.3 3.1 fusion.21
  (168 shorter events, 94.1 us)
Async XLA Ops:
  6.5 10.0 %copy-start = (bf16[2,1,8,32,1024]{4,3,2,1,0:T(8,128)(2,1)S(1)}, bf16[2,1,8,32,1024]{4,3,2,1,0:T(8,128)(2,1)}, u32[]{:S(2)}) copy-start(bf16[2,1,8,32,1024]{4,3,2,1,0:T(8,128)(2,1)} %param.12) | copy-start | bytes 3145732
  6.5 143.5 %all-gather.4.cloned.1.call-start = ((), (), s32[]{:S(2)}) async-start(), calls=%async_computation.3 | async-start | bytes 2228224 | tf_op jit(solution)/shard_map/all_gather | solution.py:147
  7.3 9.9 %copy-start.9 = (f32[2,64]{1,0:T(2,128)S(1)}, f32[2,64]{1,0:T(2,128)}, u32[]{:S(2)}) copy-start(f32[2,64]{1,0:T(2,128)} %param.16) | copy-start | bytes 1540
  7.3 206.6 %all-gather.6.cloned.1.call-start = ((), (), s32[]{:S(2)}) async-start(), calls=%async_computation.4 | async-start | bytes 6684672 | tf_op jit(solution)/shard_map/all_gather | solution.py:151
  10.0 13.7 %collective-permute-start = (bf16[2,1,6,32,1024]{4,3,2,1,0:T(8,128)(2,1)}, bf16[2,1,6,32,1024]{4,3,2,1,0:T(8,128)(2,1)S(1)}, u32[]{:S(2)}, u32[]{:S(2)}) collective-permute-start(bf16[2,1,6,32,1024]{4,3,2,1,0:T(8,128)(2,1)} %get-tuple-element.103), channel_id=1, source_target_pairs={{0,4},{4,8},{8,12},{1,5},{5,9},{9,13},{2,6},{6,10},{10,14},{3,7},{... | collective-permute-start | bytes 2359304 | tf_op jit(solution)/shard_map/ppermute | solution.py:16
  14.5 13.6 %collective-permute-start.1 = (bf16[2,1,6,32,1024]{4,3,2,1,0:T(8,128)(2,1)}, bf16[2,1,6,32,1024]{4,3,2,1,0:T(8,128)(2,1)}, u32[]{:S(2)}, u32[]{:S(2)}) collective-permute-start(bf16[2,1,6,32,1024]{4,3,2,1,0:T(8,128)(2,1)} %get-tuple-element.104), channel_id=1, source_target_pairs={{4,0},{8,4},{12,8},{5,1},{9,5},{13,9},{6,2},{10,6},{14,10},{7,3},{... | collective-permute-start | bytes 2359304 | tf_op jit(solution)/shard_map/ppermute | solution.py:19
  31.4 11.0 %collective-permute-start.2 = (bf16[2,1,20,6,1024]{4,2,3,1,0:T(8,128)(2,1)}, bf16[2,1,20,6,1024]{4,2,3,1,0:T(8,128)(2,1)}, u32[]{:S(2)}, u32[]{:S(2)}) collective-permute-start(bf16[2,1,20,6,1024]{4,2,3,1,0:T(8,128)(2,1)} %get-tuple-element.99), channel_id=1, source_target_pairs={{0,1},{1,2},{2,3},{4,5},{5,6},{6,7},{8,9},{9,10},{10,11},{12,13},{... | collective-permute-start | bytes 1474568 | tf_op jit(solution)/shard_map/ppermute | solution.py:16
  35.7 11.2 %collective-permute-start.3 = (bf16[2,1,20,6,1024]{4,2,3,1,0:T(8,128)(2,1)}, bf16[2,1,20,6,1024]{4,2,3,1,0:T(8,128)(2,1)}, u32[]{:S(2)}, u32[]{:S(2)}) collective-permute-start(bf16[2,1,20,6,1024]{4,2,3,1,0:T(8,128)(2,1)} %get-tuple-element.100), channel_id=1, source_target_pairs={{1,0},{2,1},{3,2},{5,4},{6,5},{7,6},{9,8},{10,9},{11,10},{13,12},{... | collective-permute-start | bytes 1474568 | tf_op jit(solution)/shard_map/ppermute | solution.py:19
  71.5 4.9 %copy-start.8 = (bf16[16,256,64]{1,2,0:T(8,128)(2,1)S(1)}, bf16[16,256,64]{1,2,0:T(8,128)(2,1)}, u32[]{:S(2)}) copy-start(bf16[16,256,64]{1,2,0:T(8,128)(2,1)} %custom-call) | copy-start | bytes 1572868
  76.5 73.6 %copy-start.5 = (bf16[1,8,32,1024]{3,2,1,0:T(8,128)(2,1)S(1)}, bf16[1,8,32,1024]{3,2,1,0:T(8,128)(2,1)}, u32[]{:S(2)}) copy-start(bf16[1,8,32,1024]{3,2,1,0:T(8,128)(2,1)} %param.10) | copy-start | bytes 1572868
  150.0 63.9 %copy-start.10 = (f32[1024]{0:T(1024)S(1)}, f32[1024]{0:T(1024)}, u32[]{:S(2)}) copy-start(f32[1024]{0:T(1024)} %param.14) | copy-start | bytes 12292
  152.5 65.9 %copy-start.6 = (bf16[256,1024]{1,0:T(8,128)(2,1)}, bf16[256,1024]{1,0:T(8,128)(2,1)S(1)}, u32[]{:S(2)}) copy-start(bf16[256,1024]{1,0:T(8,128)(2,1)S(1)} %get-tuple-element.108) | copy-start | bytes 1572868
  218.5 2.6 copy-start.2
  222.8 8.9 %copy-start.1 = (f32[256,1024]{1,0:T(8,128)S(1)}, f32[256,1024]{1,0:T(8,128)}, u32[]{:S(2)}) copy-start(f32[256,1024]{1,0:T(8,128)} %get-tuple-element.96) | copy-start | bytes 3145732
  225.1 20.9 %all-to-all-start.1 = ((bf16[1,1,16,16,1024]{4,3,1,0,2:T(8,128)(2,1)}), bf16[1,1,16,16,1024]{4,3,1,0,2:T(8,128)(2,1)}, u32[]{:S(2)}, u32[]{:S(2)}) async-start(bf16[1,1,16,16,1024]{4,3,1,0,2:T(8,128)(2,1)} %fusion.33), calls=%async_computation.1 | async-start | bytes 1048576 | tf_op jit(solution)/shard_map/all_to_all | solution.py:157
  233.4 1.5 copy-start.3
  246.0 30.4 %all-to-all-start = ((bf16[2,1,16,16,1024]{4,3,1,0,2:T(8,128)(2,1)}), bf16[2,1,16,16,1024]{4,3,1,0,2:T(8,128)(2,1)S(1)}, u32[]{:S(2)}, u32[]{:S(2)}) async-start(bf16[2,1,16,16,1024]{4,3,1,0,2:T(8,128)(2,1)} %copy.52), calls=%async_computation | async-start | bytes 2097152 | tf_op jit(solution)/shard_map/all_to_all | solution.py:158
  250.3 92.9 %all-gather.8.cloned.1.call-start = ((), (), s32[]{:S(2)}) async-start(), calls=%async_computation.5 | async-start | bytes 2228224 | tf_op jit(solution)/shard_map/all_gather | solution.py:163
  280.4 1.2 copy-start.4
  283.1 60.2 %copy-start.7 = (bf16[256,1024]{1,0:T(8,128)(2,1)S(1)}, bf16[256,1024]{1,0:T(8,128)(2,1)}, u32[]{:S(2)}) copy-start(bf16[256,1024]{1,0:T(8,128)(2,1)} %copy-done.6) | copy-start | bytes 1572868
  284.9 58.4 %all-to-all-start.2 = ((bf16[16,16,1024]{2,1,0:T(8,128)(2,1)}), bf16[16,16,1024]{2,1,0:T(8,128)(2,1)S(1)}, u32[]{:S(2)}, u32[]{:S(2)}) async-start(bf16[16,16,1024]{2,1,0:T(8,128)(2,1)} %reshape.267), calls=%async_computation.2 | async-start | bytes 1048576 | tf_op jit(solution)/shard_map/all_to_all | solution.py:161
Sparse Core Ops, SparseCore 0:
  9.9 86.0 all-gather.3
  98.6 115.1 all-gather.5
  253.8 89.4 all-gather.7
where the time goes:
time: 357 us; the launch traced here: 353 us
  waiting for transfers between devices  163 us (46%)
  local copies, waits for them, and re-layouts  72.6 us (20%)
  matrix products  54 us (15%)
  starting transfers between devices  27.7 us (8%)
  other arithmetic  21.7 us (6%)
  between operations  13.5 us (4%)
    all_gather x1, waiting for transfers between devices, local(): lax.all_gather(cross_input, 'view', axis=0, tiled=True)  61.3 us
    all_gather x1, waiting for transfers between devices, local(): lax.all_gather(cross_output, 'view', axis=0, tiled=True)  51.6 us
    all_to_all x1, waiting for transfers between devices, local(): lax.all_to_all(pair_block, 'view', split_axis=2, concat_axis=1, tiled=True)  23.4 us
    and x32, local copies, waits for them, and re-layouts, both_masks(): joined = by_row[:, None, :, None] & by_col[None, :, None, :]  22 us
    dot_general x16, matrix products, one_head(): jnp.dot(query_h, key_h.T, preferred_element_type=jnp.float32)  21 us
    dot_general x16, matrix products, one_head(): jnp.dot(exponent.astype(jnp.bfloat16), value_h, preferred_element_type=jn...  19.7 us
    unnamed x26, local copies, waits for them, and re-layouts  13.8 us
    dot_general x3, matrix products, row_folder(): return jnp.dot(left_rows, piece, preferred_element_type=jnp.float32)  10.3 us
  transfers between devices with their start and end apart: 10, of which 7 were waited for; matrix products, arithmetic and copies ran while one was open for 38% of the time, Pallas kernels for 0%

commit v1 on v0

v1 whole, which is shorter than its diff:
```python
import functools

import jax
import jax.numpy as jnp
from jax import lax
from jax.experimental import pallas as pl
from jax.experimental.pallas import tpu as pltpu
from jax.sharding import PartitionSpec as P

HEAD_DIM = 64
WINDOW = 13
RADIUS = 6
SIDE = 8
PAIR = 2 * HEAD_DIM
BIG = -1e9
F32 = jnp.float32
BF16 = jnp.bfloat16


def iota(shape, dim):
    return lax.broadcasted_iota(jnp.int32, shape, dim)


def attend(query, query_tags, key, key_tags, value):
    count = query.shape[0]
    low = (iota((1, PAIR), 1) < HEAD_DIM).astype(F32)
    query = query * BF16(HEAD_DIM**-0.5)
    first = query * low.astype(BF16)
    second = query * (1.0 - low).astype(BF16)
    left = jnp.concatenate(
        [
            jnp.concatenate([first, query_tags], axis=1),
            jnp.concatenate([second, query_tags], axis=1),
        ],
        axis=0,
    )
    right = jnp.concatenate([key, key_tags], axis=1)
    scores = lax.dot_general(left, right, (((1,), (1,)), ((), ())), preferred_element_type=F32)
    highest = jnp.max(scores, axis=1, keepdims=True)
    probs = jnp.exp(scores - highest).astype(BF16)
    mixed = jnp.concatenate([value, jnp.ones(value.shape, BF16)], axis=1)
    out = jnp.dot(probs, mixed, preferred_element_type=F32)
    pick = iota((count, PAIR), 1) < HEAD_DIM
    top = jnp.where(pick, out[:count, :PAIR], out[count:, :PAIR])
    below = jnp.where(pick, out[:count, PAIR:], out[count:, PAIR:])
    return top / below


def window_ok(queried, keyed, total):
    first_at = jnp.clip(queried - RADIUS, 0, total - WINDOW)
    return (keyed >= first_at) & (keyed <= first_at + WINDOW - 1)


def near_start(half, row_start, part_rows, span_rows, rows_total, held_rows):
    at = row_start + half * part_rows
    first = jnp.clip(at - RADIUS, 0, rows_total - WINDOW) - (row_start - RADIUS)
    return jnp.minimum(first, held_rows - span_rows)


def near_key_tags(half, start, row_start, col_start, part_rows, shape, rows_total, cols_total):
    lane = iota(shape, 2)
    key_row = row_start - RADIUS + start + iota(shape, 0)
    key_col = col_start - SIDE + iota(shape, 1)
    row_ok = window_ok(row_start + half * part_rows + lane, key_row, rows_total)
    col_ok = window_ok(col_start + lane - 32, key_col, cols_total)
    bad = ((lane < part_rows) & ~row_ok) | ((lane >= 32) & (lane < 64) & ~col_ok)
    return jnp.where(bad, BIG, 0.0).astype(BF16).reshape(shape[0] * shape[1], shape[2])


def near_query_tags(part_rows, cols):
    shape = (part_rows, cols, PAIR)
    lane = iota(shape, 2)
    hit = (lane == iota(shape, 0)) | (lane == 32 + iota(shape, 1))
    return jnp.where(hit, 1.0, 0.0).astype(BF16).reshape(part_rows * cols, PAIR)


def head_norm(values, gain_row, ones_block):
    squares = values * values
    upper = squares.astype(BF16)
    lower = (squares - upper.astype(F32)).astype(BF16)
    total = jnp.dot(
        jnp.concatenate([upper, lower], axis=1), ones_block, preferred_element_type=F32
    )
    return (values * lax.rsqrt(total * (1.0 / HEAD_DIM) + 1e-06) * gain_row).astype(BF16)


def near_kernel(rows_total, cols_total, query, pairs, out, key_tags):
    rows, cols, features = query.shape
    held_rows, held_cols = pairs.shape[1], pairs.shape[2]
    part_rows = rows // 2
    span_rows = part_rows + 2 * RADIUS
    row_start = lax.axis_index("row") * rows
    col_start = lax.axis_index("col") * cols
    query_tags = near_query_tags(part_rows, cols)
    part = part_rows * cols
    for half in range(2):
        start = near_start(half, row_start, part_rows, span_rows, rows_total, held_rows)
        key_tags[...] = near_key_tags(
            half, start, row_start, col_start, part_rows,
            (span_rows, held_cols, PAIR), rows_total, cols_total,
        )

        @pl.loop(0, features // PAIR)
        def _(at):
            lanes = pl.ds(pl.multiple_of(at * PAIR, PAIR), PAIR)
            queried = query[half * part_rows : (half + 1) * part_rows, :, lanes]
            key = pairs[0, pl.ds(start, span_rows), :, lanes].reshape(span_rows * held_cols, PAIR)
            value = pairs[1, pl.ds(start, span_rows), :, lanes].reshape(span_rows * held_cols, PAIR)
            result = attend(
                queried.reshape(part, PAIR), query_tags, key, key_tags[...], value
            )
            out[half * part : (half + 1) * part, lanes] = result.astype(BF16)


def cross_kernel(views, hidden, gain, weight, head_gain, last, out, normed, mixed):
    tokens, features = hidden.shape
    pixels = tokens // views
    x = hidden[...].astype(F32)
    meansq = jnp.mean(x * x, axis=1, keepdims=True)
    normed[...] = (x * lax.rsqrt(meansq + 1e-05) * gain[...]).astype(BF16)
    shape = (views, pixels, PAIR)
    same = (iota(shape, 2) == iota(shape, 1)).reshape(tokens, PAIR)
    tagged = iota(shape, 2).reshape(tokens, PAIR) < pixels
    query_tags = jnp.where(same, 1.0, 0.0).astype(BF16)
    key_tags = jnp.where(tagged & ~same, BIG, 0.0).astype(BF16)
    block = jnp.where(
        (iota((PAIR, PAIR), 0) < HEAD_DIM) == (iota((PAIR, PAIR), 1) < HEAD_DIM), 1.0, 0.0
    ).astype(BF16)
    ones_block = jnp.concatenate([block, block], axis=0)
    query_gain = jnp.concatenate([head_gain[0:1, :]] * 2, axis=1)
    key_gain = jnp.concatenate([head_gain[1:2, :]] * 2, axis=1)
    wide = 2 * PAIR

    @pl.loop(0, features // wide)
    def _(at):
        base = pl.multiple_of(at * wide, wide)
        q4, k4, v4 = (
            jnp.dot(
                normed[...], weight[:, pl.ds(part * features + base, wide)],
                preferred_element_type=F32,
            )
            for part in range(3)
        )
        for piece in range(2):
            cut = slice(piece * PAIR, (piece + 1) * PAIR)
            result = attend(
                head_norm(q4[:, cut], query_gain, ones_block), query_tags,
                head_norm(k4[:, cut], key_gain, ones_block), key_tags,
                v4[:, cut].astype(BF16),
            )
            mixed[:, pl.ds(base + piece * PAIR, PAIR)] = result.astype(BF16)

    @pl.loop(0, features // wide)
    def _(at):
        lanes = pl.ds(pl.multiple_of(at * wide, wide), wide)
        term = jnp.dot(mixed[...], last[:, lanes], preferred_element_type=F32)
        out[:, lanes] = (hidden[:, lanes].astype(F32) + term).astype(BF16)


def padded(block, sides):
    for axis, dim, width in sides:
        count = lax.axis_size(axis)
        forward = [(i, i + 1) for i in range(count - 1)]
        backward = [(target, source) for source, target in forward]
        low = lax.ppermute(
            lax.slice_in_dim(block, block.shape[dim] - width, None, axis=dim), axis, forward
        )
        high = lax.ppermute(lax.slice_in_dim(block, 0, width, axis=dim), axis, backward)
        block = jnp.concatenate([low, block, high], axis=dim)
    return block


def local(residual, window_query, window_pairs, near_output, norm_gain, cross_input, head_gain, cross_output):
    _, rows, cols, features = residual.shape
    tokens = rows * cols
    views = lax.axis_size("view")
    rows_total = rows * lax.axis_size("row")
    cols_total = cols * lax.axis_size("col")
    near_weight = lax.all_gather(near_output, "view", axis=0, tiled=True)
    in_weight = lax.all_gather(cross_input, "view", axis=0, tiled=True)
    out_weight = lax.all_gather(cross_output, "view", axis=0, tiled=True)
    nearby = padded(window_pairs[:, 0], (("row", 1, RADIUS), ("col", 2, SIDE)))
    span = (rows // 2 + 2 * RADIUS) * nearby.shape[2]
    attended = pl.pallas_call(
        functools.partial(near_kernel, rows_total, cols_total),
        out_shape=jax.ShapeDtypeStruct((tokens, features), BF16),
        in_specs=[pl.BlockSpec(memory_space=pltpu.VMEM)] * 2,
        out_specs=pl.BlockSpec(memory_space=pltpu.VMEM),
        scratch_shapes=[pltpu.VMEM((span, PAIR), BF16)],
        compiler_params=pltpu.CompilerParams(vmem_limit_bytes=48 << 20),
        name="near_attention",
    )(window_query[0], nearby)
    near_term = jnp.dot(attended, near_weight, preferred_element_type=F32)
    hidden = (residual[0].reshape(tokens, features).astype(F32) + near_term).astype(BF16)
    moved = lax.all_to_all(
        hidden.reshape(views, tokens // views, features), "view", split_axis=0, concat_axis=0, tiled=True
    ).reshape(tokens, features)
    done = pl.pallas_call(
        functools.partial(cross_kernel, views),
        out_shape=jax.ShapeDtypeStruct((tokens, features), BF16),
        in_specs=[pl.BlockSpec(memory_space=pltpu.VMEM)] * 5,
        out_specs=pl.BlockSpec(memory_space=pltpu.VMEM),
        scratch_shapes=[pltpu.VMEM((tokens, features), BF16)] * 2,
        compiler_params=pltpu.CompilerParams(vmem_limit_bytes=48 << 20),
        name="cross_attention",
    )(moved, norm_gain.reshape(1, features), in_weight, head_gain, out_weight)
    back = lax.all_to_all(
        done.reshape(views, tokens // views, features), "view", split_axis=0, concat_axis=0, tiled=True
    )
    return back.reshape(1, rows, cols, features)


def solution(mesh):
    in_specs = (
        P("view", "row", "col", None),
        P("view", "row", "col", None),
        P(None, "view", "row", "col", None),
        P("view", None),
        P(),
        P("view", None),
        P(),
        P("view", None),
    )
    out_specs = P("view", "row", "col", None)
    return jax.shard_map(local, mesh=mesh, in_specs=in_specs, out_specs=out_specs, check_vma=False)
```

time: 357 us -> 342 us (0.958)
  waiting for transfers between devices: 163 us -> 259 us
  local copies, waits for them, and re-layouts: 72.6 us -> 3.97 us
  matrix products: 54 us -> 3.11 us
  Pallas kernels: 0 us -> 23.1 us
  other arithmetic: 21.7 us -> 0.57 us
  blocking collectives: 0 us -> 20.6 us
  starting transfers between devices: 27.7 us -> 15.7 us
    all_gather x3, waiting for transfers between devices: 113 us -> 235 us  [the longest x1 118 us: local(): in_weight = lax.all_gather(cross_input, 'view', axis=0, tiled=True)]
    dot_general x37 -> x1, matrix products: 54 us -> 3.11 us  [local(): near_term = jnp.dot(attended, near_weight, preferred_element_type=F32)]
    all_to_all x3 -> x1, waiting for transfers between devices: 33.3 us -> 0.01 us  [local(): lax.all_to_all(hidden.reshape(views, tokens // views, features), 'view',...]
    pallas_call x0 -> x2, Pallas kernels: none -> 23.1 us  [the longest x1 12.6 us: local(): pl.pallas_call(functools.partial(near_kernel, rows_total, cols_total), ou...]
    and x32 -> x0, local copies, waits for them, and re-layouts: 22 us -> none  [both_masks(): joined = by_row[:, None, :, None] & by_col[None, :, None, :]]
    all_to_all x0 -> x1, blocking collectives: none -> 20.6 us  [local(): lax.all_to_all(done.reshape(views, tokens // views, features), 'view', sp...]
    another operation x7 -> x0, local copies, waits for them, and re-layouts: 19.8 us -> none  [the longest x1 5.98 us: neighborhood(): key_tile.reshape(span_total, head_count, HEAD_DIM).transpose(1, 0, 2)]
    unnamed x26 -> x13, local copies, waits for them, and re-layouts: 13.8 us -> 2.41 us
  transfers between devices with their start and end apart: 10 -> 8, of which waited for: 7 -> 7; matrix products, arithmetic and copies ran while one was open for 38% -> 2% of each run, Pallas kernels for 0% -> 4%
where the time goes in v1:
time: 342 us; the launch traced here: 339 us
  waiting for transfers between devices  259 us (76%)
  Pallas kernels  23.1 us (7%)
  blocking collectives  20.6 us (6%)
  starting transfers between devices  15.7 us (5%)
  between operations  13.2 us (4%)
  local copies, waits for them, and re-layouts  3.97 us (1%)
    all_gather x1, waiting for transfers between devices, local(): in_weight = lax.all_gather(cross_input, 'view', axis=0, tiled=True)  118 us
    all_gather x1, waiting for transfers between devices, local(): out_weight = lax.all_gather(cross_output, 'view', axis=0, tiled=True)  77.6 us
    all_gather x1, waiting for transfers between devices, local(): near_weight = lax.all_gather(near_output, 'view', axis=0, tiled=True)  39.2 us
    all_to_all x1, blocking collectives, local(): lax.all_to_all(done.reshape(views, tokens // views, features), 'view', sp...  20.6 us
    ppermute x2, waiting for transfers between devices, padded(): lax.ppermute(lax.slice_in_dim(block, block.shape[dim] - width, None, axis...  13 us
    pallas_call x1, Pallas kernels, local(): pl.pallas_call(functools.partial(near_kernel, rows_total, cols_total), ou...  12.6 us
    pallas_call x1, Pallas kernels, local(): pl.pallas_call(functools.partial(cross_kernel, views), out_shape=jax.Shap...  10.5 us
    ppermute x2, waiting for transfers between devices, padded(): lax.ppermute(lax.slice_in_dim(block, 0, width, axis=dim), axis, backward)  9.09 us
  transfers between devices with their start and end apart: 8, of which 7 were waited for; matrix products, arithmetic and copies ran while one was open for 2% of the time, Pallas kernels for 4%

profile of v1, /device:TPU:1, one launch (start us, length us, event | category | flops | bytes accessed | tf_op | source)
XLA Modules:
  0.0 339.0 jit_solution(15086107281961432420)
XLA Ops:
  6.5 0.0 all-gather.4.cloned.1.call-start
  6.5 0.7 all-gather.4.cloned.1.call-update
  7.3 0.0 all-gather.8.cloned.1.call-start
  7.3 0.7 all-gather.8.cloned.1.call-update
  8.0 0.0 all-gather.6.cloned.1.call-start
  8.1 0.7 all-gather.6.cloned.1.call-update
  8.7 1.6 fusion.1
  10.3 4.5 %collective-permute-start = (bf16[2,6,32,1024]{3,2,1,0:T(8,128)(2,1)S(1)}, bf16[2,6,32,1024]{3,2,1,0:T(8,128)(2,1)S(1)}, u32[]{:S(2)}, u32[]{:S(2)}) collective-permute-start(bf16[2,6,32,1024]{3,2,1,0:T(8,128)(2,1)S(1)} %get-tuple-element.7), channel_id=1, source_target_pairs={{0,4},{4,8},{8,12},{1,5},{5,9},{9,13},{2,6},{6,10},{10,14},{3,7},{... | collective-permute-start | bytes 2359304 | tf_op jit(solution)/shard_map/ppermute | solution.py:165
  14.8 2.0 collective-permute-start.1
  16.8 6.9 %collective-permute-done = bf16[2,6,32,1024]{3,2,1,0:T(8,128)(2,1)S(1)} collective-permute-done((bf16[2,6,32,1024]{3,2,1,0:T(8,128)(2,1)S(1)}, bf16[2,6,32,1024]{3,2,1,0:T(8,128)(2,1)S(1)}, u32[]{:S(2)}, u32[]{:S(2)}) %collective-permute-start) | collective-permute-done | bytes 786464 | tf_op jit(solution)/shard_map/ppermute | solution.py:165
  23.7 4.7 %collective-permute-done.1 = bf16[2,6,32,1024]{3,2,1,0:T(8,128)(2,1)S(1)} collective-permute-done((bf16[2,6,32,1024]{3,2,1,0:T(8,128)(2,1)S(1)}, bf16[2,6,32,1024]{3,2,1,0:T(8,128)(2,1)S(1)}, u32[]{:S(2)}, u32[]{:S(2)}) %collective-permute-start.1) | collective-permute-done | bytes 786464 | tf_op jit(solution)/shard_map/ppermute | solution.py:168
  28.4 0.1 pad_maximum_fusion.3
  28.6 3.2 collective-permute-start.2
  31.8 0.0 copy-start.1
  31.8 1.4 collective-permute-start.3
  33.2 6.0 %collective-permute-done.2 = bf16[2,20,8,1024]{3,2,1,0:T(8,128)(2,1)S(1)} collective-permute-done((bf16[2,20,8,1024]{3,2,1,0:T(8,128)(2,1)S(1)}, bf16[2,20,8,1024]{3,2,1,0:T(8,128)(2,1)S(1)}, u32[]{:S(2)}, u32[]{:S(2)}) %collective-permute-start.2) | collective-permute-done | bytes 655392 | tf_op jit(solution)/shard_map/ppermute | solution.py:165
  39.3 4.4 %collective-permute-done.3 = bf16[2,20,8,1024]{3,2,1,0:T(8,128)(2,1)S(1)} collective-permute-done((bf16[2,20,8,1024]{3,2,1,0:T(8,128)(2,1)S(1)}, bf16[2,20,8,1024]{3,2,1,0:T(8,128)(2,1)S(1)}, u32[]{:S(2)}, u32[]{:S(2)}) %collective-permute-start.3) | collective-permute-done | bytes 655392 | tf_op jit(solution)/shard_map/ppermute | solution.py:168
  43.7 0.5 pad_maximum_fusion.pairs
  44.1 0.0 copy-start.5
  44.2 0.0 copy-start.2
  44.2 0.0 copy-start.3
  44.2 12.6 %near_attention.1 = bf16[256,1024]{1,0:T(8,128)(2,1)S(1)} custom-call(bf16[8,32,1024]{2,1,0:T(8,128)(2,1)S(1)} %bitcast.13, bf16[2,20,48,1024]{3,2,1,0:T(8,128)(2,1)S(1)} %pad_maximum_fusion.pairs), custom_call_target="tpu_custom_call" | custom-call | tf_op jit(solution)/shard_map/near_attention/pallas_call | solution.py:184
  56.8 39.2 %all-gather.4.cloned.1.call-done = bf16[1024,1024]{1,0:T(8,128)(2,1)} async-done(((bf16[64,1024]{1,0:T(8,128)(2,1)}), bf16[1024,1024]{1,0:T(8,128)(2,1)}) %all-gather.4.cloned.1.call-update) | async-done | bytes 2097168 | tf_op jit(solution)/shard_map/all_gather | solution.py:179
  96.0 3.1 fusion
  99.1 4.5 %all-to-all-start = ((bf16[16,16,1024]{2,1,0:T(8,128)(2,1)}), bf16[16,16,1024]{2,1,0:T(8,128)(2,1)S(1)}, u32[]{:S(2)}, u32[]{:S(2)}) async-start(bf16[16,16,1024]{2,1,0:T(8,128)(2,1)} %bitcast.3), calls=%async_computation | async-start | bytes 1048576 | tf_op jit(solution)/shard_map/all_to_all | solution.py:195
  103.6 77.6 %all-gather.8.cloned.1.call-done.last = bf16[1024,1024]{1,0:T(8,128)(2,1)} async-done(((bf16[64,1024]{1,0:T(8,128)(2,1)}), bf16[1024,1024]{1,0:T(8,128)(2,1)}) %all-gather.8.cloned.1.call-update) | async-done | bytes 2097168 | tf_op jit(solution)/shard_map/all_gather | solution.py:181
  181.2 0.0 all-to-all-done
  181.2 117.8 %all-gather.6.cloned.1.call-done.weight = bf16[1024,3072]{1,0:T(8,128)(2,1)} async-done(((bf16[64,3072]{1,0:T(8,128)(2,1)}), bf16[1024,3072]{1,0:T(8,128)(2,1)}) %all-gather.6.cloned.1.call-update) | async-done | bytes 6291472 | tf_op jit(solution)/shard_map/all_gather | solution.py:180
  299.1 1.6 copy-done
  300.6 10.5 %cross_attention.1 = bf16[256,1024]{1,0:T(8,128)(2,1)S(1)} custom-call(bf16[256,1024]{1,0:T(8,128)(2,1)S(1)} %bitcast.11, f32[1,1024]{1,0:T(1,128)S(1)} %bitcast.14, bf16[1024,3072]{1,0:T(8,128)(2,1)} %all-gather.6.cloned.1.call-done.weight, f32[2,64]{1,0:T(2,128)S(1)} %copy-done.3, bf16[1024,1024]{1,0:T(8,128)(2,1)S(1)} %copy-done), custom_call_target="tpu_custom_call" | custom-call | tf_op jit(solution)/shard_map/cross_attention/pallas_call | solution.py:198
  311.1 20.6 %all_to_all.10 = bf16[16,16,1024]{2,1,0:T(8,128)(2,1)S(1)} all-to-all(bf16[16,16,1024]{2,1,0:T(8,128)(2,1)S(1)} %bitcast.12), channel_id=1, replica_groups=mesh['view'=16,'row'=4,'col'=4] {'view'}, dimensions={0} | all-to-all | bytes 1048576 | tf_op jit(solution)/shard_map/all_to_all | solution.py:207
  331.7 0.8 copy.10
  (7 shorter events, 0.0 us)
Async XLA Ops:
  6.5 21.9 %copy-start.4 = (bf16[2,1,8,32,1024]{4,3,2,1,0:T(8,128)(2,1)S(1)}, bf16[2,1,8,32,1024]{4,3,2,1,0:T(8,128)(2,1)}, u32[]{:S(2)}) copy-start(bf16[2,1,8,32,1024]{4,3,2,1,0:T(8,128)(2,1)} %param.10) | copy-start | bytes 3145732
  6.5 89.5 %all-gather.4.cloned.1.call-start = ((), (), s32[]{:S(2)}) async-start(), calls=%async_computation.2 | async-start | bytes 2228224 | tf_op jit(solution)/shard_map/all_gather | solution.py:179
  7.3 174.0 %all-gather.8.cloned.1.call-start = ((), (), s32[]{:S(2)}) async-start(), calls=%async_computation.4 | async-start | bytes 2228224 | tf_op jit(solution)/shard_map/all_gather | solution.py:181
  8.0 291.0 %all-gather.6.cloned.1.call-start = ((), (), s32[]{:S(2)}) async-start(), calls=%async_computation.3 | async-start | bytes 6684672 | tf_op jit(solution)/shard_map/all_gather | solution.py:180
  10.3 13.4 %collective-permute-start = (bf16[2,6,32,1024]{3,2,1,0:T(8,128)(2,1)S(1)}, bf16[2,6,32,1024]{3,2,1,0:T(8,128)(2,1)S(1)}, u32[]{:S(2)}, u32[]{:S(2)}) collective-permute-start(bf16[2,6,32,1024]{3,2,1,0:T(8,128)(2,1)S(1)} %get-tuple-element.7), channel_id=1, source_target_pairs={{0,4},{4,8},{8,12},{1,5},{5,9},{9,13},{2,6},{6,10},{10,14},{3,7},{... | collective-permute-start | bytes 2359304 | tf_op jit(solution)/shard_map/ppermute | solution.py:165
  14.8 13.6 %collective-permute-start.1 = (bf16[2,6,32,1024]{3,2,1,0:T(8,128)(2,1)S(1)}, bf16[2,6,32,1024]{3,2,1,0:T(8,128)(2,1)S(1)}, u32[]{:S(2)}, u32[]{:S(2)}) collective-permute-start(bf16[2,6,32,1024]{3,2,1,0:T(8,128)(2,1)S(1)} %get-tuple-element.8), channel_id=1, source_target_pairs={{4,0},{8,4},{12,8},{5,1},{9,5},{13,9},{6,2},{10,6},{14,10},{7,3},{... | collective-permute-start | bytes 2359304 | tf_op jit(solution)/shard_map/ppermute | solution.py:168
  28.6 10.7 %collective-permute-start.2 = (bf16[2,20,8,1024]{3,2,1,0:T(8,128)(2,1)S(1)}, bf16[2,20,8,1024]{3,2,1,0:T(8,128)(2,1)S(1)}, u32[]{:S(2)}, u32[]{:S(2)}) collective-permute-start(bf16[2,20,8,1024]{3,2,1,0:T(8,128)(2,1)S(1)} %get-tuple-element.5), channel_id=1, source_target_pairs={{0,1},{1,2},{2,3},{4,5},{5,6},{6,7},{8,9},{9,10},{10,11},{12,13},{... | collective-permute-start | bytes 1966088 | tf_op jit(solution)/shard_map/ppermute | solution.py:165
  31.8 12.4 %copy-start.1 = (bf16[1,8,32,1024]{3,2,1,0:T(8,128)(2,1)S(1)}, bf16[1,8,32,1024]{3,2,1,0:T(8,128)(2,1)}, u32[]{:S(2)}) copy-start(bf16[1,8,32,1024]{3,2,1,0:T(8,128)(2,1)} %param.9) | copy-start | bytes 1572868
  31.8 11.9 %collective-permute-start.3 = (bf16[2,20,8,1024]{3,2,1,0:T(8,128)(2,1)S(1)}, bf16[2,20,8,1024]{3,2,1,0:T(8,128)(2,1)S(1)}, u32[]{:S(2)}, u32[]{:S(2)}) collective-permute-start(bf16[2,20,8,1024]{3,2,1,0:T(8,128)(2,1)S(1)} %get-tuple-element.6), channel_id=1, source_target_pairs={{1,0},{2,1},{3,2},{5,4},{6,5},{7,6},{9,8},{10,9},{11,10},{13,12},{... | collective-permute-start | bytes 1966088 | tf_op jit(solution)/shard_map/ppermute | solution.py:168
  44.1 51.9 %copy-start.5 = (bf16[1,8,32,1024]{3,2,1,0:T(8,128)(2,1)S(1)}, bf16[1,8,32,1024]{3,2,1,0:T(8,128)(2,1)}, u32[]{:S(2)}) copy-start(bf16[1,8,32,1024]{3,2,1,0:T(8,128)(2,1)} %param.8) | copy-start | bytes 1572868
  44.2 254.9 %copy-start.2 = (f32[1024]{0:T(1024)S(1)}, f32[1024]{0:T(1024)}, u32[]{:S(2)}) copy-start(f32[1024]{0:T(1024)} %param.12) | copy-start | bytes 12292
  44.2 254.9 %copy-start.3 = (f32[2,64]{1,0:T(2,128)S(1)}, f32[2,64]{1,0:T(2,128)}, u32[]{:S(2)}) copy-start(f32[2,64]{1,0:T(2,128)} %head_gain.1) | copy-start | bytes 1540
  99.1 82.1 %all-to-all-start = ((bf16[16,16,1024]{2,1,0:T(8,128)(2,1)}), bf16[16,16,1024]{2,1,0:T(8,128)(2,1)S(1)}, u32[]{:S(2)}, u32[]{:S(2)}) async-start(bf16[16,16,1024]{2,1,0:T(8,128)(2,1)} %bitcast.3), calls=%async_computation | async-start | bytes 1048576 | tf_op jit(solution)/shard_map/all_to_all | solution.py:195
  299.1 1.6 copy-start
Sparse Core Ops, SparseCore 0:
  9.9 86.0 all-gather.3
  98.6 82.5 all-gather.7
  183.8 115.1 all-gather.5
